TPU v7x, 32 devices: a whole 2x2x4 slice. The times are simulated.
32 devices in a mesh: grid: 8 (over z, y), tile: 4 (over x, core).
Axes of the slice: x: 2, y: 2, z: 4, core: 2. Of those that a mesh axis runs over, the one named last changes fastest.
Arguments:
- point_values: bfloat16 [256, 16384], P('grid', 'tile'), may hold values from -1.75 to 1.75
- sig_blocks: int32 [8, 16], P('grid'), may hold values from 0 to 31, as said below
- density: bfloat16 [16384, 16384], P('grid', 'tile'), may hold values from -0.0625 to 0.0625
- coulomb_core: bfloat16 [512, 512], replicated, may hold values from -0.25 to 0.25
- screen_mask: int32 [32, 32], replicated, may hold values 0 or 1
- ao_centers: float32 [3, 16384], replicated, may hold values from -1 to 1
- ao_widths: float32 [16384], replicated, may hold values from 0.25 to 1
- point_coords: float32 [3, 256], P(None, 'grid'), may hold values from -1 to 1
- lmo_coeffs: bfloat16 [16384, 1024], P('tile'), may hold values from -0.0625 to 0.0625
- domain_blocks: int32 [4, 16], replicated, may hold values from 0 to 31, as said below
Outputs:
- half: bfloat16 [1024, 16384], P('tile', 'grid')
Inputs may be any that keep to these rules, and one draw needn't show every extreme that they name: `sig_blocks`: each batch names 16 different AO blocks. `domain_blocks`: each strip's 16 blocks are different, and every AO block lies in the domain of some strip.
All inputs are finite; a program needn't handle non-finite values.
Results may differ from a plain program's by a relative error of at most 0.02.
Values may be sent and summed in bfloat16 or wider, within the bound.
A program may use at most 128 MiB of HBM per device.

v0:
```python
import jax
import jax.numpy as jnp
from jax import lax
from jax.sharding import PartitionSpec as P

highest = lax.Precision.HIGHEST


def kernel_weights(ao_centers, ao_widths, point_coords):
    offsets = ao_centers[:, None, :] - point_coords[:, :, None]
    return 1.0 / jnp.sqrt(jnp.sum(offsets * offsets, axis=0) + ao_widths[None, :])


def spread_mask(flag_rows, batch_points, block_size):
    batches, block_count = flag_rows.shape
    expanded = jnp.broadcast_to(
        flag_rows[:, None, :, None], (batches, batch_points, block_count, block_size)
    )
    return expanded.reshape(batches * batch_points, block_count * block_size)


def shards(
    point_values,
    sig_blocks,
    density,
    coulomb_core,
    screen_mask,
    ao_centers,
    ao_widths,
    point_coords,
    lmo_coeffs,
    domain_blocks,
):
    grid_count = lax.axis_size("grid")
    panel_index = lax.axis_index("tile")
    batches = sig_blocks.shape[0]
    own_rows, own_cols = density.shape
    points = point_values.shape[0]
    batch_points = points // batches
    block_size = coulomb_core.shape[0]
    total_aos = ao_widths.shape[0]
    all_blocks = total_aos // block_size
    col_blocks = own_cols // block_size
    row_blocks = own_rows // block_size
    block_ids = jnp.arange(all_blocks, dtype=jnp.int32)
    named_blocks = jnp.any(sig_blocks[:, :, None] == block_ids[None, None, :], axis=1).astype(
        jnp.float32
    )
    first_col = panel_index * col_blocks
    named_cols = lax.dynamic_slice_in_dim(named_blocks, first_col, col_blocks, 1)
    col_mask = spread_mask(named_cols, batch_points, block_size)
    masked_local = point_values * col_mask.astype(jnp.bfloat16)
    dest_named = jnp.max(named_blocks.reshape(batches, grid_count, row_blocks), axis=2)
    outgoing = masked_local.reshape(batches, batch_points, 1, own_cols) * dest_named[
        :, None, :, None
    ].astype(jnp.bfloat16)
    product = jnp.einsum(
        "bpgc,rc->bpgr",
        lax.all_to_all(outgoing, "grid", split_axis=2, concat_axis=2, tiled=True),
        density,
        preferred_element_type=jnp.float32,
    )
    arrivals = lax.all_to_all(
        product.astype(jnp.bfloat16), "grid", split_axis=2, concat_axis=2, tiled=True
    )
    row_mask = spread_mask(named_blocks, batch_points, block_size)
    partial_term = arrivals.reshape(points, total_aos).astype(jnp.float32) * row_mask
    coefficient = kernel_weights(ao_centers, ao_widths, point_coords)
    core_float = coulomb_core.astype(jnp.float32)
    screen_float = screen_mask.astype(jnp.float32)
    density_term = lax.psum(partial_term.astype(jnp.bfloat16), "tile").astype(jnp.float32)
    weighted = (coefficient * density_term).reshape(points, all_blocks, block_size)
    screen_rows = lax.dynamic_slice_in_dim(screen_float, first_col, col_blocks, 0)
    screened = jnp.einsum("kj,pja->pka", screen_rows, weighted, precision=highest)
    kernel_part = jnp.einsum(
        "ab,pkb->pka", core_float, screened, preferred_element_type=jnp.float32
    ).reshape(points, own_cols)
    coeff_cols = lax.dynamic_slice_in_dim(coefficient, panel_index * own_cols, own_cols, 1)
    potential = (coeff_cols * kernel_part * col_mask).astype(jnp.bfloat16)
    potential_out = jnp.broadcast_to(
        potential.reshape(batches, batch_points, 1, own_cols),
        (batches, batch_points, grid_count, own_cols),
    )
    whole_points = lax.all_gather(masked_local, "tile", axis=1, tiled=True)
    row_values, col_values = (
        lax.all_to_all(
            whole_points.reshape(batches, batch_points, grid_count, own_rows),
            "grid",
            split_axis=2,
            concat_axis=2,
            tiled=True,
        ),
        lax.all_to_all(potential_out, "grid", split_axis=2, concat_axis=2, tiled=True),
    )
    exch_tile = jnp.einsum(
        "bpgr,bpgc->rc", row_values, col_values, preferred_element_type=jnp.float32
    ).astype(jnp.bfloat16)
    number_of_slabs = domain_blocks.shape[0]
    localized_orbital_total = lmo_coeffs.shape[1]
    strip_width = localized_orbital_total // number_of_slabs
    local_ids = first_col + jnp.arange(col_blocks, dtype=jnp.int32)
    in_domain = jnp.any(domain_blocks[:, :, None] == local_ids[None, None, :], axis=1)
    domain_flags = jnp.transpose(in_domain)
    domain_mask = jnp.broadcast_to(
        domain_flags[:, None, :, None], (col_blocks, block_size, number_of_slabs, strip_width)
    ).reshape(own_cols, localized_orbital_total)
    region_expansion_factor = lmo_coeffs * domain_mask.astype(jnp.bfloat16)
    return lax.psum_scatter(
        lax.dot_general(
            region_expansion_factor,
            exch_tile,
            (((0,), (1,)), ((), ())),
            preferred_element_type=jnp.float32,
        ).astype(jnp.bfloat16),
        "tile",
        scatter_dimension=0,
        tiled=True,
    )


def solution(mesh):
    in_specs = (
        P("grid", "tile"),
        P("grid", None),
        P("grid", "tile"),
        P(),
        P(),
        P(),
        P(),
        P(None, "grid"),
        P("tile", None),
        P(),
    )
    out_specs = P("tile", "grid")
    return jax.shard_map(shards, mesh=mesh, in_specs=in_specs, out_specs=out_specs, check_vma=False)
```

profile of v0, /device:TPU:0, one launch (start us, length us, event | category | flops | bytes accessed | tf_op | source)
XLA Modules:
  0.0 288.2 jit_solution(9041671634119760462)
XLA Ops:
  6.5 0.8 fusion.26
  7.7 1.0 broadcast_multiply_fusion.1
  8.9 55.3 %all_to_all.20 = bf16[1,32,8,4096]{3,1,0,2:T(8,128)(2,1)S(1)} all-to-all(bf16[1,32,8,4096]{3,1,0,2:T(8,128)(2,1)S(1)} %broadcast_multiply_fusion), channel_id=1, replica_groups=mesh['grid'=8,'tile'=4] {'grid'}, dimensions={2} | all-to-all | bytes 4194304 | tf_op jit(solution)/shard_map/all_to_all | solution.py:59
  64.3 9.6 %fusion.11 = bf16[1,32,8,2048]{3,2,1,0:T(8,128)(2,1)} fusion(bf16[2048,4096]{1,0:T(8,128)(2,1)} %param.12, bf16[1,32,8,4096]{3,1,0,2:T(8,128)(2,1)S(1)} %all_to_all.20), kind=kOutput, calls=%fused_computation.9 | convolution fusion | flops 4295491584 | bytes 19922944 | tf_op jit(solution)/shard_map/bpgc,rc->bpgr/dot_general | solution.py:57
  73.8 2.8 copy.25
  76.6 3.6 %all-to-all-start.2 = ((bf16[1,32,8,2048]{3,1,0,2:T(8,128)(2,1)}), bf16[1,32,8,2048]{3,1,0,2:T(8,128)(2,1)S(1)}, u32[]{:S(2)}, u32[]{:S(2)}) async-start(bf16[1,32,8,2048]{3,1,0,2:T(8,128)(2,1)} %copy.25), calls=%async_computation.2 | async-start | bytes 2097152 | tf_op jit(solution)/shard_map/all_to_all | solution.py:63
  81.1 24.7 %all-to-all-done.2 = bf16[1,32,8,2048]{3,1,0,2:T(8,128)(2,1)S(1)} async-done(((bf16[1,32,8,2048]{3,1,0,2:T(8,128)(2,1)}), bf16[1,32,8,2048]{3,1,0,2:T(8,128)(2,1)S(1)}, u32[]{:S(2)}, u32[]{:S(2)}) %all-to-all-start.2) | async-done | bytes 1048608 | tf_op jit(solution)/shard_map/all_to_all | solution.py:63
  106.0 1.1 multiply_convert_fusion
  107.2 0.8 multiply_reduce_fusion
  108.0 1.8 copy.30
  109.9 1.6 copy.22
  111.5 4.2 %all-to-all-start = ((bf16[1,32,8,2048]{3,1,0,2:T(8,128)(2,1)}), bf16[1,32,8,2048]{3,1,0,2:T(8,128)(2,1)}, u32[]{:S(2)}, u32[]{:S(2)}) async-start(bf16[1,32,8,2048]{3,1,0,2:T(8,128)(2,1)} %copy.22), calls=%async_computation | async-start | bytes 2097152 | tf_op jit(solution)/shard_map/all_to_all | solution.py:86
  115.7 26.8 %all-reduce.2.cloned.1.call-done = bf16[32,16384]{1,0:T(8,128)(2,1)} async-done(((bf16[32,16384]{1,0:T(8,128)(2,1)}), bf16[32,16384]{1,0:T(8,128)(2,1)}) %all-reduce.2.cloned.1.call-update) | async-done | bytes 1048592 | tf_op jit(solution)/shard_map/psum | solution.py:71
  142.5 1.5 convert_multiply_fusion
  144.0 1.2 copy.33
  145.2 1.9 convolution_bitcast_fusion
  147.9 1.6 broadcast_in_dim.49
  149.5 5.9 %all-to-all-start.3 = ((bf16[1,32,8,4096]{3,1,0,2:T(8,128)(2,1)}), bf16[1,32,8,4096]{3,1,0,2:T(8,128)(2,1)S(1)}, u32[]{:S(2)}, u32[]{:S(2)}) async-start(bf16[1,32,8,4096]{3,1,0,2:T(8,128)(2,1)} %broadcast_in_dim.49), calls=%async_computation.3 | async-start | bytes 4194304 | tf_op jit(solution)/shard_map/all_to_all | solution.py:93
  156.0 2.2 broadcast_in_dim.18
  158.2 4.0 %copy.28 = pred[512,8,4,256]{3,1,2,0:T(8,128)(4,1)} copy(pred[512,8,4,256]{3,2,1,0:T(4,128)(4,1)S(1)} %bitcast.72) | data formatting | bytes 8388608
  162.3 40.5 %all-to-all-done.3 = bf16[1,32,8,4096]{3,1,0,2:T(8,128)(2,1)S(1)} async-done(((bf16[1,32,8,4096]{3,1,0,2:T(8,128)(2,1)}), bf16[1,32,8,4096]{3,1,0,2:T(8,128)(2,1)S(1)}, u32[]{:S(2)}, u32[]{:S(2)}) %all-to-all-start.3) | async-done | bytes 2097184 | tf_op jit(solution)/shard_map/all_to_all | solution.py:93
  202.8 10.0 %bitcast_convert_fusion.clone.7 = bf16[2048,4096]{1,0:T(8,128)(2,1)} fusion(bf16[1,32,8,4096]{3,1,0,2:T(8,128)(2,1)S(1)} %all-to-all-done.3, bf16[1,32,8,2048]{3,1,0,2:T(8,128)(2,1)} %all-to-all-done), kind=kOutput, calls=%fused_computation.clone.clone.clone.clone.clone.2 | convolution fusion | flops 4303355904 | bytes 19922944 | tf_op jit(solution)/shard_map/bpgr,bpgc->rc/dot_general | solution.py:95
  212.8 25.2 %fusion.5 = bf16[1024,2048]{1,0:T(8,128)(2,1)} fusion(pred[4096,1024]{1,0:T(8,128)(4,1)} %bitcast.77, bf16[4096,1024]{1,0:T(8,128)(2,1)} %param.18, bf16[2048,4096]{1,0:T(8,128)(2,1)} %bitcast_convert_fusion.clone.7), kind=kOutput, calls=%fused_computation.7 | convolution fusion | flops 17186160640 | bytes 33554432 | tf_op jit(solution)/shard_map/dot_general | solution.py:109
  237.9 43.7 %reduce-scatter.2.cloned.1.call-done = bf16[256,2048]{1,0:T(8,128)(2,1)} async-done(((bf16[1024,2048]{1,0:T(8,128)(2,1)}), bf16[256,2048]{1,0:T(8,128)(2,1)}) %reduce-scatter.2.cloned.1.call-update) | async-done | bytes 1048592 | tf_op jit(solution)/shard_map/reduce_scatter | solution.py:108
  (39 shorter events, 3.0 us)
Async XLA Ops:
  6.5 140.6 %copy-start = (bf16[512,512]{1,0:T(8,128)(2,1)S(1)}, bf16[512,512]{1,0:T(8,128)(2,1)}, u32[]{:S(2)}) copy-start(bf16[512,512]{1,0:T(8,128)(2,1)} %param.13) | copy-start | bytes 1572868
  8.7 55.6 %copy-start.2 = (bf16[32,4096]{1,0:T(8,128)(2,1)}, bf16[32,4096]{1,0:T(8,128)(2,1)S(1)}, u32[]{:S(2)}) copy-start(bf16[32,4096]{1,0:T(8,128)(2,1)S(1)} %broadcast_multiply_fusion.1) | copy-start | bytes 786436
  76.6 29.2 %all-to-all-start.2 = ((bf16[1,32,8,2048]{3,1,0,2:T(8,128)(2,1)}), bf16[1,32,8,2048]{3,1,0,2:T(8,128)(2,1)S(1)}, u32[]{:S(2)}, u32[]{:S(2)}) async-start(bf16[1,32,8,2048]{3,1,0,2:T(8,128)(2,1)} %copy.25), calls=%async_computation.2 | async-start | bytes 2097152 | tf_op jit(solution)/shard_map/all_to_all | solution.py:63
  80.2 27.8 %all-gather.2.cloned.1.call-start = ((), (), s32[]{:S(2)}) async-start(), calls=%async_computation.5 | async-start | bytes 1310720 | tf_op jit(solution)/shard_map/all_gather | solution.py:84
  80.9 61.6 %all-reduce.2.cloned.1.call-start = ((), (), s32[]{:S(2)}) async-start(), calls=%async_computation.6 | async-start | bytes 2097152 | tf_op jit(solution)/shard_map/psum | solution.py:71
  106.0 1.2 copy-start.3
  106.0 1.2 copy-start.6
  109.8 32.6 %copy-start.4 = (f32[16384]{0:T(1024)S(1)}, f32[16384]{0:T(1024)}, u32[]{:S(2)}) copy-start(f32[16384]{0:T(1024)} %param.16) | copy-start | bytes 196612
  111.5 36.4 %all-to-all-start = ((bf16[1,32,8,2048]{3,1,0,2:T(8,128)(2,1)}), bf16[1,32,8,2048]{3,1,0,2:T(8,128)(2,1)}, u32[]{:S(2)}, u32[]{:S(2)}) async-start(bf16[1,32,8,2048]{3,1,0,2:T(8,128)(2,1)} %copy.22), calls=%async_computation | async-start | bytes 2097152 | tf_op jit(solution)/shard_map/all_to_all | solution.py:86
  149.5 6.2 %copy-start.5 = (s32[4,16]{1,0:T(4,128)S(1)}, s32[4,16]{1,0:T(4,128)}, u32[]{:S(2)}) copy-start(s32[4,16]{1,0:T(4,128)} %param.19) | copy-start | bytes 772
  149.5 53.3 %all-to-all-start.3 = ((bf16[1,32,8,4096]{3,1,0,2:T(8,128)(2,1)}), bf16[1,32,8,4096]{3,1,0,2:T(8,128)(2,1)S(1)}, u32[]{:S(2)}, u32[]{:S(2)}) async-start(bf16[1,32,8,4096]{3,1,0,2:T(8,128)(2,1)} %broadcast_in_dim.49), calls=%async_computation.3 | async-start | bytes 4194304 | tf_op jit(solution)/shard_map/all_to_all | solution.py:93
  155.4 126.2 %reduce-scatter.2.cloned.1.call-start = ((), (), s32[]{:S(2)}) async-start(), calls=%async_computation.7 | async-start | bytes 5242880 | tf_op jit(solution)/shard_map/reduce_scatter | solution.py:108
  237.9 43.7 %copy-start.1 = (bf16[512,512]{1,0:T(8,128)(2,1)S(1)}, bf16[512,512]{1,0:T(8,128)(2,1)}, u32[]{:S(2)}) copy-start(bf16[512,512]{1,0:T(8,128)(2,1)} %param.13) | copy-start | bytes 1572868
Sparse Core Ops, SparseCore 0:
  82.6 18.0 all-gather.1
  107.3 35.1 all-reduce.1
  238.1 43.5 reduce-scatter.1
where the time goes:
time: 289 us; the launch traced here: 288 us
  waiting for transfers between devices  136 us (47%)
  blocking collectives  55.3 us (19%)
  matrix products  46.9 us (16%)
  local copies, waits for them, and re-layouts  16.3 us (6%)
  starting transfers between devices  14 us (5%)
  between operations  13.3 us (5%)
  other arithmetic  5.85 us (2%)
    all_to_all x1, blocking collectives, shards(): lax.all_to_all(outgoing, 'grid', split_axis=2, concat_axis=2, tiled=True)  55.3 us
    reduce_scatter x1, waiting for transfers between devices, shards(): lax.psum_scatter(lax.dot_general(region_expansion_factor, exch_tile, (((0...  43.7 us
    all_to_all x1, waiting for transfers between devices, shards(): lax.all_to_all(potential_out, 'grid', split_axis=2, concat_axis=2, tiled=...  40.5 us
    psum x1, waiting for transfers between devices, shards(): lax.psum(partial_term.astype(jnp.bfloat16), 'tile').astype(jnp.float32)  26.8 us
    dot_general x1, matrix products, shards(): lax.dot_general(region_expansion_factor, exch_tile, (((0,), (1,)), ((), (...  25.2 us
    all_to_all x1, waiting for transfers between devices, shards(): lax.all_to_all(product.astype(jnp.bfloat16), 'grid', split_axis=2, concat...  24.7 us
    dot_general x1, matrix products, shards(): jnp.einsum('bpgr,bpgc->rc', row_values, col_values, preferred_element_typ...  9.96 us
    dot_general x1, matrix products, shards(): jnp.einsum('bpgc,rc->bpgr', lax.all_to_all(outgoing, 'grid', split_axis=2...  9.56 us
  transfers between devices with their start and end apart: 6, of which 4 were waited for; matrix products, arithmetic and copies ran while one was open for 6% of the time, Pallas kernels for 0%

commit v1 on v0

--- a/solution.py
+++ b/solution.py
@@ -68,7 +68,9 @@
     coefficient = kernel_weights(ao_centers, ao_widths, point_coords)
     core_float = coulomb_core.astype(jnp.float32)
     screen_float = screen_mask.astype(jnp.float32)
-    density_term = lax.psum(partial_term.astype(jnp.bfloat16), "tile").astype(jnp.float32)
+    density_term = jnp.sum(
+        lax.all_gather(partial_term.astype(jnp.bfloat16), "tile"), axis=0
+    ).astype(jnp.float32)
     weighted = (coefficient * density_term).reshape(points, all_blocks, block_size)
     screen_rows = lax.dynamic_slice_in_dim(screen_float, first_col, col_blocks, 0)
     screened = jnp.einsum("kj,pja->pka", screen_rows, weighted, precision=highest)

time: 289 us -> 291 us (level)
  other arithmetic: 5.85 us -> 9.32 us
  local copies, waits for them, and re-layouts: 16.3 us -> 19.5 us
  waiting for transfers between devices: 136 us -> 133 us
    psum x1 -> x0, waiting for transfers between devices: 26.8 us -> none  [shards(): lax.psum(partial_term.astype(jnp.bfloat16), 'tile').astype(jnp.float32)]
    all_gather x0 -> x1, waiting for transfers between devices: none -> 22.3 us  [shards(): lax.all_gather(partial_term.astype(jnp.bfloat16), 'tile')]
    reduce_sum x0 -> x1, other arithmetic: none -> 4.15 us  [shards(): jnp.sum(lax.all_gather(partial_term.astype(jnp.bfloat16), 'tile'), axis=0)]
    unnamed x23 -> x25, local copies, waits for them, and re-layouts: 7.83 us -> 10.8 us
  transfers between devices with their start and end apart: 6 -> 6, of which waited for: 4 -> 4; matrix products, arithmetic and copies ran while one was open for 6% -> 8% of each run, Pallas kernels for 0% -> 0%
where the time goes in v1:
time: 291 us
  waiting for transfers between devices  133 us (46%)
  blocking collectives  55.3 us (19%)
  matrix products  46.9 us (16%)
  local copies, waits for them, and re-layouts  19.5 us (7%)
  starting transfers between devices  13.8 us (5%)
  between operations  13.3 us (5%)
  other arithmetic  9.32 us (3%)
    all_to_all x1, blocking collectives, shards(): lax.all_to_all(outgoing, 'grid', split_axis=2, concat_axis=2, tiled=True)  55.3 us
    reduce_scatter x1, waiting for transfers between devices, shards(): lax.psum_scatter(lax.dot_general(region_expansion_factor, exch_tile, (((0...  42.9 us
    all_to_all x1, waiting for transfers between devices, shards(): lax.all_to_all(potential_out, 'grid', split_axis=2, concat_axis=2, tiled=...  42 us
    dot_general x1, matrix products, shards(): lax.dot_general(region_expansion_factor, exch_tile, (((0,), (1,)), ((), (...  25.2 us
    all_to_all x1, waiting for transfers between devices, shards(): lax.all_to_all(product.astype(jnp.bfloat16), 'grid', split_axis=2, concat...  24.7 us
    all_gather x1, waiting for transfers between devices, shards(): lax.all_gather(partial_term.astype(jnp.bfloat16), 'tile')  22.3 us
    unnamed x25, local copies, waits for them, and re-layouts  10.8 us
    dot_general x1, matrix products, shards(): jnp.einsum('bpgr,bpgc->rc', row_values, col_values, preferred_element_typ...  10 us
  transfers between devices with their start and end apart: 6, of which 4 were waited for; matrix products, arithmetic and copies ran while one was open for 8% of the time, Pallas kernels for 0%

profile of v1, /device:TPU:0, one launch (start us, length us, event | category | flops | bytes accessed | tf_op | source)
XLA Modules:
  0.0 290.7 jit_solution(5526961850751369359)
XLA Ops:
  6.5 0.8 fusion.31
  7.7 1.0 broadcast_multiply_fusion.1
  8.9 55.3 %all_to_all.20 = bf16[1,32,8,4096]{3,1,0,2:T(8,128)(2,1)S(1)} all-to-all(bf16[1,32,8,4096]{3,1,0,2:T(8,128)(2,1)S(1)} %broadcast_multiply_fusion), channel_id=1, replica_groups=mesh['grid'=8,'tile'=4] {'grid'}, dimensions={2} | all-to-all | bytes 4194304 | tf_op jit(solution)/shard_map/all_to_all | solution.py:59
  64.3 9.6 %fusion.11 = bf16[1,32,8,2048]{3,2,1,0:T(8,128)(2,1)} fusion(bf16[2048,4096]{1,0:T(8,128)(2,1)} %param.12, bf16[1,32,8,4096]{3,1,0,2:T(8,128)(2,1)S(1)} %all_to_all.20), kind=kOutput, calls=%fused_computation.9 | convolution fusion | flops 4295491584 | bytes 19922944 | tf_op jit(solution)/shard_map/bpgc,rc->bpgr/dot_general | solution.py:57
  73.8 2.8 copy.25
  76.6 3.6 %all-to-all-start.2 = ((bf16[1,32,8,2048]{3,1,0,2:T(8,128)(2,1)}), bf16[1,32,8,2048]{3,1,0,2:T(8,128)(2,1)S(1)}, u32[]{:S(2)}, u32[]{:S(2)}) async-start(bf16[1,32,8,2048]{3,1,0,2:T(8,128)(2,1)} %copy.25), calls=%async_computation.2 | async-start | bytes 2097152 | tf_op jit(solution)/shard_map/all_to_all | solution.py:63
  81.1 24.7 %all-to-all-done.2 = bf16[1,32,8,2048]{3,1,0,2:T(8,128)(2,1)S(1)} async-done(((bf16[1,32,8,2048]{3,1,0,2:T(8,128)(2,1)}), bf16[1,32,8,2048]{3,1,0,2:T(8,128)(2,1)S(1)}, u32[]{:S(2)}, u32[]{:S(2)}) %all-to-all-start.2) | async-done | bytes 1048608 | tf_op jit(solution)/shard_map/all_to_all | solution.py:63
  106.3 1.1 multiply_convert_fusion
  108.3 2.5 copy.32
  110.8 1.8 copy.31
  112.6 1.6 copy.22
  114.2 4.4 %all-to-all-start = ((bf16[1,32,8,2048]{3,1,0,2:T(8,128)(2,1)}), bf16[1,32,8,2048]{3,1,0,2:T(8,128)(2,1)}, u32[]{:S(2)}, u32[]{:S(2)}) async-start(bf16[1,32,8,2048]{3,1,0,2:T(8,128)(2,1)} %copy.22), calls=%async_computation | async-start | bytes 2097152 | tf_op jit(solution)/shard_map/all_to_all | solution.py:88
  118.6 22.3 %all-gather.5.cloned.1.call-done = bf16[4,32,16384]{2,1,0:T(8,128)(2,1)} async-done(((bf16[1,32,16384]{2,1,0:T(8,128)(2,1)}), bf16[4,32,16384]{2,1,0:T(8,128)(2,1)}) %all-gather.5.cloned.1.call-update) | async-done | bytes 4194320 | tf_op jit(solution)/shard_map/all_gather | solution.py:72
  140.9 4.2 %reduce_sum.25 = bf16[32,16384]{1,0:T(8,128)(2,1)} reduce(bf16[4,32,16384]{2,1,0:T(8,128)(2,1)} %all-gather.5.cloned.1.call-done, bf16[]{:T(256)} %constant.5.clone.1), dimensions={0}, to_apply=%region_4.0 | reduce | flops 1572864 | bytes 5242882 | tf_op jit(solution)/shard_map/reduce_sum | solution.py:71
  145.0 1.7 copy.34
  147.5 1.9 convolution_bitcast_fusion
  150.2 1.6 broadcast_in_dim.49
  151.8 5.6 %all-to-all-start.3 = ((bf16[1,32,8,4096]{3,1,0,2:T(8,128)(2,1)}), bf16[1,32,8,4096]{3,1,0,2:T(8,128)(2,1)S(1)}, u32[]{:S(2)}, u32[]{:S(2)}) async-start(bf16[1,32,8,4096]{3,1,0,2:T(8,128)(2,1)} %broadcast_in_dim.49), calls=%async_computation.3 | async-start | bytes 4194304 | tf_op jit(solution)/shard_map/all_to_all | solution.py:95
  157.9 2.2 broadcast_in_dim.18
  160.1 4.1 %copy.29 = pred[512,8,4,256]{3,1,2,0:T(8,128)(4,1)} copy(pred[512,8,4,256]{3,2,1,0:T(4,128)(4,1)S(1)} %bitcast.79) | data formatting | bytes 8388608
  164.2 42.0 %all-to-all-done.3 = bf16[1,32,8,4096]{3,1,0,2:T(8,128)(2,1)S(1)} async-done(((bf16[1,32,8,4096]{3,1,0,2:T(8,128)(2,1)}), bf16[1,32,8,4096]{3,1,0,2:T(8,128)(2,1)S(1)}, u32[]{:S(2)}, u32[]{:S(2)}) %all-to-all-start.3) | async-done | bytes 2097184 | tf_op jit(solution)/shard_map/all_to_all | solution.py:95
  206.1 10.0 %bitcast_convert_fusion.clone.7 = bf16[2048,4096]{1,0:T(8,128)(2,1)} fusion(bf16[1,32,8,4096]{3,1,0,2:T(8,128)(2,1)S(1)} %all-to-all-done.3, bf16[1,32,8,2048]{3,1,0,2:T(8,128)(2,1)} %all-to-all-done), kind=kOutput, calls=%fused_computation.clone.clone.clone.clone.clone.2 | convolution fusion | flops 4303355904 | bytes 19922944 | tf_op jit(solution)/shard_map/bpgr,bpgc->rc/dot_general | solution.py:97
  216.1 25.2 %fusion.5 = bf16[1024,2048]{1,0:T(8,128)(2,1)} fusion(pred[4096,1024]{1,0:T(8,128)(4,1)} %bitcast.82, bf16[4096,1024]{1,0:T(8,128)(2,1)} %param.18, bf16[2048,4096]{1,0:T(8,128)(2,1)} %bitcast_convert_fusion.clone.7), kind=kOutput, calls=%fused_computation.7 | convolution fusion | flops 17186160640 | bytes 33554432 | tf_op jit(solution)/shard_map/dot_general | solution.py:111
  241.3 42.9 %reduce-scatter.2.cloned.1.call-done = bf16[256,2048]{1,0:T(8,128)(2,1)} async-done(((bf16[1024,2048]{1,0:T(8,128)(2,1)}), bf16[256,2048]{1,0:T(8,128)(2,1)}) %reduce-scatter.2.cloned.1.call-update) | async-done | bytes 1048592 | tf_op jit(solution)/shard_map/reduce_scatter | solution.py:110
  (47 shorter events, 4.6 us)
Async XLA Ops:
  6.5 142.9 %copy-start = (bf16[512,512]{1,0:T(8,128)(2,1)S(1)}, bf16[512,512]{1,0:T(8,128)(2,1)}, u32[]{:S(2)}) copy-start(bf16[512,512]{1,0:T(8,128)(2,1)} %param.13) | copy-start | bytes 1572868
  8.7 55.6 %copy-start.3 = (bf16[32,4096]{1,0:T(8,128)(2,1)}, bf16[32,4096]{1,0:T(8,128)(2,1)S(1)}, u32[]{:S(2)}) copy-start(bf16[32,4096]{1,0:T(8,128)(2,1)S(1)} %broadcast_multiply_fusion.1) | copy-start | bytes 786436
  76.6 29.2 %all-to-all-start.2 = ((bf16[1,32,8,2048]{3,1,0,2:T(8,128)(2,1)}), bf16[1,32,8,2048]{3,1,0,2:T(8,128)(2,1)S(1)}, u32[]{:S(2)}, u32[]{:S(2)}) async-start(bf16[1,32,8,2048]{3,1,0,2:T(8,128)(2,1)} %copy.25), calls=%async_computation.2 | async-start | bytes 2097152 | tf_op jit(solution)/shard_map/all_to_all | solution.py:63
  80.2 30.6 %all-gather.3.cloned.1.call-start = ((), (), s32[]{:S(2)}) async-start(), calls=%async_computation.5 | async-start | bytes 1310720 | tf_op jit(solution)/shard_map/all_gather | solution.py:86
  80.9 60.0 %all-gather.5.cloned.1.call-start = ((), (), s32[]{:S(2)}) async-start(), calls=%async_computation.6 | async-start | bytes 5242880 | tf_op jit(solution)/shard_map/all_gather | solution.py:72
  106.2 1.2 copy-start.5
  106.2 1.2 copy-start.4
  106.3 1.2 copy-start.7
  114.2 36.0 %all-to-all-start = ((bf16[1,32,8,2048]{3,1,0,2:T(8,128)(2,1)}), bf16[1,32,8,2048]{3,1,0,2:T(8,128)(2,1)}, u32[]{:S(2)}, u32[]{:S(2)}) async-start(bf16[1,32,8,2048]{3,1,0,2:T(8,128)(2,1)} %copy.22), calls=%async_computation | async-start | bytes 2097152 | tf_op jit(solution)/shard_map/all_to_all | solution.py:88
  145.0 1.9 copy-start.2
  147.5 2.6 dynamic-slice-start
  151.8 5.7 %copy-start.6 = (s32[4,16]{1,0:T(4,128)S(1)}, s32[4,16]{1,0:T(4,128)}, u32[]{:S(2)}) copy-start(s32[4,16]{1,0:T(4,128)} %param.19) | copy-start | bytes 772
  151.8 54.3 %all-to-all-start.3 = ((bf16[1,32,8,4096]{3,1,0,2:T(8,128)(2,1)}), bf16[1,32,8,4096]{3,1,0,2:T(8,128)(2,1)S(1)}, u32[]{:S(2)}, u32[]{:S(2)}) async-start(bf16[1,32,8,4096]{3,1,0,2:T(8,128)(2,1)} %broadcast_in_dim.49), calls=%async_computation.3 | async-start | bytes 4194304 | tf_op jit(solution)/shard_map/all_to_all | solution.py:95
  157.5 126.7 %reduce-scatter.2.cloned.1.call-start = ((), (), s32[]{:S(2)}) async-start(), calls=%async_computation.7 | async-start | bytes 5242880 | tf_op jit(solution)/shard_map/reduce_scatter | solution.py:110
  241.3 42.9 %copy-start.1 = (bf16[512,512]{1,0:T(8,128)(2,1)S(1)}, bf16[512,512]{1,0:T(8,128)(2,1)}, u32[]{:S(2)}) copy-start(bf16[512,512]{1,0:T(8,128)(2,1)} %param.13) | copy-start | bytes 1572868
Sparse Core Ops, SparseCore 0:
  82.6 18.0 all-gather.2
  107.5 33.2 all-gather.4
  241.4 42.7 reduce-scatter.1
